TPU v7x, 128 devices: a whole 4x4x4 slice. The times are simulated.
128 devices in a mesh: expert: 64 (over x, y, z), dp: 2 (over core).
Axes of the slice: x: 4, y: 4, z: 4, core: 2. Of those that a mesh axis runs over, the one named last changes fastest.
Arguments:
- tokens: bfloat16 [12288, 4096], P(('expert', 'dp')), may hold values from -6 to 6
- w_gate: bfloat16 [128, 4096, 768], P(('expert', 'dp')), may hold values from -0.09375 to 0.09375
- w_up: bfloat16 [128, 4096, 768], P(('expert', 'dp')), may hold values from -0.09375 to 0.09375
- w_down: bfloat16 [128, 768, 4096], P(('expert', 'dp')), may hold values from -0.21875 to 0.21875
- route_ids: int32 [12288, 8], P(('expert', 'dp')), may hold values from 0 to 127, all different within a row
- route_gates: float32 [12288, 8], P(('expert', 'dp')), may hold values from 0.05 to 0.4
- hot_experts: int32 [1], replicated, may hold values from 0 to 127
Outputs:
- mixed: bfloat16 [12288, 4096], P(('expert', 'dp'))
Inputs may be any that keep to these rules, and one draw needn't show every extreme that they name: `route_ids`: each row names 8 different experts.
All inputs are finite; a program needn't handle non-finite values.
Results may differ from a plain program's by a relative error of at most 0.007.
Values may be sent and summed in bfloat16 or wider, within the bound.
A program may use at most 192 MiB of HBM per device.

v0:
```python
import jax
import jax.numpy as jnp
from jax import lax
from jax.sharding import PartitionSpec as P

CAP = 6


def expert_ffn(in_rows, gate_w, up_w, down_w):
    gate_val = jnp.dot(in_rows, gate_w, preferred_element_type=jnp.float32)
    up_val = jnp.dot(in_rows, up_w, preferred_element_type=jnp.float32)
    hidden = (jax.nn.silu(gate_val) * up_val).astype(jnp.bfloat16)
    return jnp.dot(hidden, down_w, preferred_element_type=jnp.float32).astype(jnp.bfloat16)


def on_device(tokens, w_gate, w_up, w_down, route_ids, route_gates, hot_experts):
    feat_width = tokens.shape[1]
    tok_rows = tokens.shape[0]
    top_k = route_ids.shape[1]
    n_dp = lax.axis_size("dp")
    experts = lax.axis_size("expert") * n_dp
    hot_id = hot_experts[0]
    me = lax.axis_index("expert") * n_dp + lax.axis_index("dp")
    own = (w_gate[0], w_up[0], w_down[0])
    with jax.named_scope("hot_weight_broadcast"):
        is_root = me == hot_id
        hot_w = tuple(
            (lax.psum(jnp.where(is_root, w, jnp.zeros_like(w)), ("expert", "dp")) for w in own)
        )
    with jax.named_scope("routing"):
        flat_ids = route_ids.reshape(-1)
        labels = lax.iota(jnp.int32, experts)
        onehot = (flat_ids[:, None] == labels[None, :]).astype(jnp.int32)
        rank_of = jnp.sum(onehot * (jnp.cumsum(onehot, axis=0) - 1), axis=1)
        is_kept = (flat_ids != hot_id) & (rank_of < CAP)
        slot_of = jnp.where(is_kept, flat_ids * CAP + rank_of, experts * CAP)
        slots = lax.iota(jnp.int32, experts * CAP)
        hit = slot_of[None, :] == slots[:, None]
        dispatch = jnp.any(hit.reshape(experts * CAP, tok_rows, top_k), axis=2)
    with jax.named_scope("dispatch"):
        outgoing = jnp.dot(
            dispatch.astype(tokens.dtype), tokens, preferred_element_type=jnp.float32
        ).astype(tokens.dtype)
        to_send = outgoing.reshape(experts, CAP * feat_width)
        arrived = lax.all_to_all(to_send, ("expert", "dp"), 0, 0, tiled=True)
    with jax.named_scope("expert_ffn"):
        results = expert_ffn(arrived.reshape(-1, feat_width), *own)
    with jax.named_scope("return"):
        come_back = lax.all_to_all(
            results.reshape(experts, CAP * feat_width), ("expert", "dp"), 0, 0, tiled=True
        )
        returned = come_back.reshape(experts * CAP, feat_width)
    with jax.named_scope("combine"):
        gate_flat = route_gates.reshape(-1)
        cold_weight = jnp.where(is_kept, gate_flat, jnp.zeros_like(gate_flat))
        weight_of_slot = jnp.where(hit, cold_weight[None, :], 0.0)
        combine = jnp.sum(weight_of_slot.reshape(experts * CAP, tok_rows, top_k), axis=2).T
        cold_sum = jnp.dot(
            combine,
            returned.astype(jnp.float32),
            precision=lax.Precision.HIGHEST,
            preferred_element_type=jnp.float32,
        )
    with jax.named_scope("hot_expert"):
        hot_out = expert_ffn(tokens, *hot_w)
        hot_weight = jnp.sum(
            jnp.where(route_ids == hot_id, route_gates, jnp.zeros_like(route_gates)), axis=1
        )
        combined = cold_sum + hot_weight[:, None] * hot_out.astype(jnp.float32)
    return combined.astype(jnp.bfloat16)


def solution(mesh):
    in_specs = (
        P(("expert", "dp"), None),
        P(("expert", "dp"), None, None),
        P(("expert", "dp"), None, None),
        P(("expert", "dp"), None, None),
        P(("expert", "dp"), None),
        P(("expert", "dp"), None),
        P(),
    )
    out_specs = P(("expert", "dp"), None)
    return jax.shard_map(
        on_device, mesh=mesh, in_specs=in_specs, out_specs=out_specs, check_vma=False
    )
```

profile of v0, /device:TPU:0, one launch (start us, length us, event | category | flops | bytes accessed | tf_op | source)
XLA Modules:
  0.0 559.9 jit_solution(3620452224844530923)
XLA Ops:
  10.8 4.5 convolution_convert_fusion
  15.2 23.8 %all_to_all.16 = bf16[128,1,24576]{2,1,0:T(2,128)(2,1)} reshape(bf16[768,4096]{1,0:T(8,128)(2,1)} %convolution_convert_fusion) | data formatting | bytes 12582912 | tf_op jit(solution)/shard_map/dispatch/all_to_all | solution.py:45
  39.4 38.9 %reduce.2 = bf16[128,24576]{1,0:T(8,128)(2,1)} reduce(bf16[128,1,24576]{2,1,0:T(2,128)(2,1)} %all_to_all.16, bf16[]{:T(256)} %broadcast.85), dimensions={1}, to_apply=%all_to_all.16.reduce_sub_computation | reduce | bytes 12582914 | tf_op jit(solution)/shard_map/dispatch/all_to_all | solution.py:45
  78.3 9.4 %reshape.90 = bf16[128,2,12288]{2,1,0:T(2,128)(2,1)} reshape(bf16[128,24576]{1,0:T(8,128)(2,1)} %reduce.2) | data formatting | bytes 12582912
  87.7 11.6 %all-to-all-start = ((bf16[128,2,12288]{2,1,0:T(2,128)(2,1)}), bf16[128,2,12288]{2,1,0:T(2,128)(2,1)}, u32[]{:S(2)}, u32[]{:S(2)}) async-start(bf16[128,2,12288]{2,1,0:T(2,128)(2,1)} %reshape.90), calls=%async_computation | async-start | bytes 12582912 | tf_op jit(solution)/shard_map/dispatch/all_to_all | solution.py:45
  99.4 5.9 %bitcast_select_fusion = bf16[768,4096]{1,0:T(8,128)(2,1)} fusion(bf16[1,768,4096]{2,1,0:T(8,128)(2,1)} %param.10, pred[]{:T(512)S(6)} %eq.59), kind=kLoop, calls=%fused_computation.2 | loop fusion | flops 3145728 | bytes 12582913 | tf_op jit(solution)/shard_map/hot_weight_broadcast/jit(_where)/select_n | solution.py:28
  105.3 9.9 %bitcast_select_fusion.1 = (bf16[4096,768]{1,0:T(8,128)(2,1)}, bf16[4096,768]{1,0:T(8,128)(2,1)}) fusion(bf16[1,4096,768]{2,1,0:T(8,128)(2,1)} %param.9, pred[]{:T(512)S(6)} %eq.59, bf16[1,4096,768]{2,1,0:T(8,128)(2,1)} %param.8), kind=kLoop, calls=%fused_computation.4 | loop fusion | flops 6291456 | bytes 25165824 | tf_op jit(solution)/shard_map/hot_weight_broadcast/jit(_where)/select_n | solution.py:28
  115.1 65.2 %all-to-all-done = bf16[128,2,12288]{2,1,0:T(2,128)(2,1)} async-done(((bf16[128,2,12288]{2,1,0:T(2,128)(2,1)}), bf16[128,2,12288]{2,1,0:T(2,128)(2,1)}, u32[]{:S(2)}, u32[]{:S(2)}) %all-to-all-start) | async-done | bytes 6291488 | tf_op jit(solution)/shard_map/dispatch/all_to_all | solution.py:45
  180.4 34.5 %reshape.91 = bf16[128,1,24576]{2,1,0:T(2,128)(2,1)} reshape(bf16[128,2,12288]{2,1,0:T(2,128)(2,1)} %all-to-all-done) | data formatting | bytes 12582912
  214.8 38.3 %reduce = bf16[128,24576]{1,0:T(8,128)(2,1)} reduce(bf16[128,1,24576]{2,1,0:T(2,128)(2,1)} %reshape.91, bf16[]{:T(256)} %constant.43), dimensions={1}, to_apply=%all_to_all.13.reduce_sub_computation | reduce | bytes 12582914 | tf_op jit(solution)/shard_map/dispatch/all_to_all | solution.py:45
  253.2 11.2 %reshape.86 = bf16[768,4096]{1,0:T(8,128)(2,1)} reshape(bf16[128,24576]{1,0:T(8,128)(2,1)} %reduce) | data formatting | bytes 12582912 | tf_op jit(solution)/shard_map/expert_ffn/reshape | solution.py:47
  264.4 9.1 %fusion.3 = f32[768,768]{1,0:T(8,128)S(1)} fusion(bf16[768,4096]{1,0:T(8,128)(2,1)} %reshape.86, bf16[1,4096,768]{2,1,0:T(8,128)(2,1)} %param.8), kind=kOutput, calls=%fused_computation.8 | convolution fusion | flops 4831838208 | bytes 14942208 | tf_op jit(solution)/shard_map/expert_ffn/dot_general | solution.py:10
  273.5 8.0 %multiply_convert_fusion = bf16[768,768]{1,0:T(8,128)(2,1)S(1)} fusion(f32[768,768]{1,0:T(8,128)S(1)} %fusion.3, bf16[768,4096]{1,0:T(8,128)(2,1)S(1)} %copy-done.1, bf16[1,4096,768]{2,1,0:T(8,128)(2,1)} %param.9), kind=kOutput, calls=%fused_computation.15 | convolution fusion | flops 4835377152 | bytes 16121856 | tf_op jit(solution)/shard_map/expert_ffn/dot_general | solution.py:11
  281.6 7.1 %convolution_convert_fusion.1 = bf16[768,4096]{1,0:T(8,128)(2,1)} fusion(bf16[768,768]{1,0:T(8,128)(2,1)S(1)} %multiply_convert_fusion, bf16[1,768,4096]{2,1,0:T(8,128)(2,1)S(1)} %bitcast.50), kind=kOutput, calls=%fused_computation.1 | convolution fusion | flops 4834983936 | bytes 13762560 | tf_op jit(solution)/shard_map/expert_ffn/dot_general | solution.py:13
  288.7 23.9 %all_to_all.17 = bf16[128,1,24576]{2,1,0:T(2,128)(2,1)} reshape(bf16[768,4096]{1,0:T(8,128)(2,1)} %convolution_convert_fusion.1) | data formatting | bytes 12582912 | tf_op jit(solution)/shard_map/return/all_to_all | solution.py:49
  312.5 38.8 %reduce.3 = bf16[128,24576]{1,0:T(8,128)(2,1)} reduce(bf16[128,1,24576]{2,1,0:T(2,128)(2,1)} %all_to_all.17, bf16[]{:T(256)} %broadcast.85), dimensions={1}, to_apply=%all_to_all.17.reduce_sub_computation | reduce | bytes 12582914 | tf_op jit(solution)/shard_map/return/all_to_all | solution.py:49
  351.4 9.7 %reshape.92 = bf16[128,2,12288]{2,1,0:T(2,128)(2,1)} reshape(bf16[128,24576]{1,0:T(8,128)(2,1)} %reduce.3) | data formatting | bytes 12582912
  361.1 7.8 %all-to-all-start.1 = ((bf16[128,2,12288]{2,1,0:T(2,128)(2,1)}), bf16[128,2,12288]{2,1,0:T(2,128)(2,1)}, u32[]{:S(2)}, u32[]{:S(2)}) async-start(bf16[128,2,12288]{2,1,0:T(2,128)(2,1)} %reshape.92), calls=%async_computation.1 | async-start | bytes 12582912 | tf_op jit(solution)/shard_map/return/all_to_all | solution.py:49
  369.8 81.9 %all-reduce.3.cloned.1.call-done = (bf16[768,4096]{1,0:T(8,128)(2,1)}, bf16[4096,768]{1,0:T(8,128)(2,1)}, bf16[4096,768]{1,0:T(8,128)(2,1)}) async-done(((bf16[768,4096]{1,0:T(8,128)(2,1)}, bf16[4096,768]{1,0:T(8,128)(2,1)}, bf16[4096,768]{1,0:T(8,128)(2,1)}), (bf16[768,4096]{1,0:T(8,128)(2,1)}, bf16[4096,768]{1,0:T(8,128)(2,1)}, bf16[4096,768]{1,0:T(8,128)(2,1)})) %all-reduce.3.cloned.1.call-update) | async-done | bytes 18874384 | tf_op jit(solution)/shard_map/hot_weight_broadcast/psum | solution.py:28
  455.6 7.1 %fusion.7 = f32[96,4096]{1,0:T(8,128)S(1)} fusion(bf16[768,4096]{1,0:T(8,128)(2,1)} %get-tuple-element.5, bf16[96,4096]{1,0:T(8,128)(2,1)S(1)} %copy-done, bf16[4096,768]{1,0:T(8,128)(2,1)} %get-tuple-element.6, f32[96]{0:T(128)S(1)} %get-tuple-element.9, f32[96,768]{1,0:T(8,128)S(1)} %convolution_bitcast_fusion.1), kind=kOutput, calls=%fused_computation.14 | convolution fusion | flops 1209581568 | bytes 15237504 | tf_op jit(solution)/shard_map/hot_expert/dot_general | solution.py:13
  462.8 33.8 %reshape.93 = bf16[128,1,24576]{2,1,0:T(2,128)(2,1)} reshape(bf16[128,2,12288]{2,1,0:T(2,128)(2,1)} %all-to-all-done.1) | data formatting | bytes 12582912
  496.6 38.3 %reduce.1 = bf16[128,24576]{1,0:T(8,128)(2,1)} reduce(bf16[128,1,24576]{2,1,0:T(2,128)(2,1)} %reshape.93, bf16[]{:T(256)} %constant.43), dimensions={1}, to_apply=%all_to_all.15.reduce_sub_computation | reduce | bytes 12582914 | tf_op jit(solution)/shard_map/return/all_to_all | solution.py:49
  534.9 11.1 %reshape.87 = bf16[768,4096]{1,0:T(8,128)(2,1)} reshape(bf16[128,24576]{1,0:T(8,128)(2,1)} %reduce.1) | data formatting | bytes 12582912 | tf_op jit(solution)/shard_map/return/reshape | solution.py:52
  546.0 6.8 %fusion.5 = bf16[96,4096]{1,0:T(8,128)(2,1)} fusion(f32[96,4096]{1,0:T(8,128)S(1)} %fusion.7, f32[768,96]{0,1:T(8,128)S(1)} %select_reduce_fusion, bf16[768,4096]{1,0:T(8,128)(2,1)} %reshape.87), kind=kOutput, calls=%fused_computation.11 | convolution fusion | flops 3624665088 | bytes 8945664 | tf_op jit(solution)/shard_map/combine/dot_general | solution.py:58
  (36 shorter events, 8.9 us)
Async XLA Ops:
  6.5 4.2 copy-start
  87.7 92.7 %all-to-all-start = ((bf16[128,2,12288]{2,1,0:T(2,128)(2,1)}), bf16[128,2,12288]{2,1,0:T(2,128)(2,1)}, u32[]{:S(2)}, u32[]{:S(2)}) async-start(bf16[128,2,12288]{2,1,0:T(2,128)(2,1)} %reshape.90), calls=%async_computation | async-start | bytes 12582912 | tf_op jit(solution)/shard_map/dispatch/all_to_all | solution.py:45
  99.3 352.4 %all-reduce.3.cloned.1.call-start = ((), (), s32[]{:S(2)}) async-start(), calls=%async_computation.2 | async-start | bytes 37748736 | tf_op jit(solution)/shard_map/hot_weight_broadcast/psum | solution.py:28
  253.2 28.4 %slice-start = ((s8[6291456]{0:T(1024)(128)(4,1)}), s8[2097152]{0:T(1024)(128)(4,1)S(1)}, s32[]{:S(2)}) async-start(s8[6291456]{0:T(1024)(128)(4,1)} %bitcast.49), calls=%async_computation.3 | async-start | bytes 4194304
  264.4 9.1 %copy-start.1 = (bf16[768,4096]{1,0:T(8,128)(2,1)S(1)}, bf16[768,4096]{1,0:T(8,128)(2,1)}, u32[]{:S(2)}) copy-start(bf16[768,4096]{1,0:T(8,128)(2,1)} %reshape.86) | copy-start | bytes 18874372
  264.4 17.2 %slice-start.1 = ((s8[6291456]{0:T(1024)(128)(4,1)}), s8[4194304]{0:T(1024)(128)(4,1)S(1)}, s32[]{:S(2)}) async-start(s8[6291456]{0:T(1024)(128)(4,1)} %bitcast.49), calls=%async_computation.4 | async-start | bytes 8388608
  361.1 7.8 %copy-start.2 = (s32[96,8]{0,1:T(8,128)S(1)}, s32[96,8]{0,1:T(8,128)}, u32[]{:S(2)}) copy-start(s32[96,8]{0,1:T(8,128)} %param.11) | copy-start | bytes 9220
  361.1 7.8 %copy-start.3 = (f32[96,8]{0,1:T(8,128)S(1)}, f32[96,8]{0,1:T(8,128)}, u32[]{:S(2)}) copy-start(f32[96,8]{0,1:T(8,128)} %param.12) | copy-start | bytes 9220
  361.1 101.7 %all-to-all-start.1 = ((bf16[128,2,12288]{2,1,0:T(2,128)(2,1)}), bf16[128,2,12288]{2,1,0:T(2,128)(2,1)}, u32[]{:S(2)}, u32[]{:S(2)}) async-start(bf16[128,2,12288]{2,1,0:T(2,128)(2,1)} %reshape.92), calls=%async_computation.1 | async-start | bytes 12582912 | tf_op jit(solution)/shard_map/return/all_to_all | solution.py:49
Sparse Core Ops, SparseCore 0:
  115.3 336.3 all-reduce.2
where the time goes:
time: 571 us; the launch traced here: 560 us
  other arithmetic  173 us (30%)
  local copies, waits for them, and re-layouts  159 us (28%)
  waiting for transfers between devices  147 us (26%)
  matrix products  46.5 us (8%)
  starting transfers between devices  19.5 us (3%)
  between operations  14.5 us (3%)
    unnamed x17, local copies, waits for them, and re-layouts  88.2 us
    psum x1, waiting for transfers between devices, on_device(): lax.psum(jnp.where(is_root, w, jnp.zeros_like(w)), ('expert', 'dp'))  81.9 us
    all_to_all x2, other arithmetic, on_device(): arrived = lax.all_to_all(to_send, ('expert', 'dp'), 0, 0, tiled=True)  77.2 us
    all_to_all x2, other arithmetic, on_device(): lax.all_to_all(results.reshape(experts, CAP * feat_width), ('expert', 'dp...  77.2 us
    all_to_all x1, waiting for transfers between devices, on_device(): arrived = lax.all_to_all(to_send, ('expert', 'dp'), 0, 0, tiled=True)  65.2 us
    all_to_all x2, local copies, waits for them, and re-layouts, on_device(): arrived = lax.all_to_all(to_send, ('expert', 'dp'), 0, 0, tiled=True)  24.2 us
    all_to_all x1, local copies, waits for them, and re-layouts, on_device(): lax.all_to_all(results.reshape(experts, CAP * feat_width), ('expert', 'dp...  23.9 us
    select_n x2, other arithmetic, on_device(): jnp.where(is_root, w, jnp.zeros_like(w))  15.8 us
  transfers between devices with their start and end apart: 3, of which 2 were waited for; matrix products, arithmetic and copies ran while one was open for 33% of the time, Pallas kernels for 0%

commit v1 on v0

--- a/solution.py
+++ b/solution.py
@@ -25,7 +25,10 @@
     with jax.named_scope("hot_weight_broadcast"):
         is_root = me == hot_id
         hot_w = tuple(
-            (lax.psum(jnp.where(is_root, w, jnp.zeros_like(w)), ("expert", "dp")) for w in own)
+            (
+                lax.psum(lax.psum(jnp.where(is_root, w, jnp.zeros_like(w)), "dp"), "expert")
+                for w in own
+            )
         )
     with jax.named_scope("routing"):
         flat_ids = route_ids.reshape(-1)

time: 571 us -> 649 us (1.14)
  blocking collectives: 0 us -> 90 us
  starting transfers between devices: 19.5 us -> 8.54 us
    all_to_all x0 -> x1, blocking collectives: none -> 90 us  [on_device(): arrived = lax.all_to_all(to_send, ('expert', 'dp'), 0, 0, tiled=True)]
    all_to_all x1, waiting for transfers between devices: 0.01 us -> 74.8 us  [on_device(): lax.all_to_all(results.reshape(experts, CAP * feat_width), ('expert', 'dp...]
    all_to_all x1 -> x0, waiting for transfers between devices: 65.2 us -> none  [on_device(): arrived = lax.all_to_all(to_send, ('expert', 'dp'), 0, 0, tiled=True)]
    all_to_all x1 -> x0, starting transfers between devices: 11.6 us -> none  [on_device(): arrived = lax.all_to_all(to_send, ('expert', 'dp'), 0, 0, tiled=True)]
    psum x1 -> x2, waiting for transfers between devices: 81.9 us -> 71.1 us  [the longest x1 71.1 us: on_device(): lax.psum(jnp.where(is_root, w, jnp.zeros_like(w)), 'dp')]
  transfers between devices with their start and end apart: 3 -> 3, of which waited for: 2 -> 2; matrix products, arithmetic and copies ran while one was open for 33% -> 46% of each run, Pallas kernels for 0% -> 0%
where the time goes in v1:
time: 649 us; the launch traced here: 637 us
  other arithmetic  172 us (27%)
  local copies, waits for them, and re-layouts  159 us (24%)
  waiting for transfers between devices  146 us (22%)
  blocking collectives  90 us (14%)
  matrix products  46.9 us (7%)
  between operations  14.5 us (2%)
  starting transfers between devices  8.54 us (1%)
    all_to_all x1, blocking collectives, on_device(): arrived = lax.all_to_all(to_send, ('expert', 'dp'), 0, 0, tiled=True)  90 us
    unnamed x17, local copies, waits for them, and re-layouts  87.2 us
    all_to_all x2, other arithmetic, on_device(): arrived = lax.all_to_all(to_send, ('expert', 'dp'), 0, 0, tiled=True)  77.1 us
    all_to_all x2, other arithmetic, on_device(): lax.all_to_all(results.reshape(experts, CAP * feat_width), ('expert', 'dp...  77.1 us
    all_to_all x1, waiting for transfers between devices, on_device(): lax.all_to_all(results.reshape(experts, CAP * feat_width), ('expert', 'dp...  74.8 us
    psum x1, waiting for transfers between devices, on_device(): lax.psum(jnp.where(is_root, w, jnp.zeros_like(w)), 'dp')  71.1 us
    all_to_all x2, local copies, waits for them, and re-layouts, on_device(): arrived = lax.all_to_all(to_send, ('expert', 'dp'), 0, 0, tiled=True)  24.4 us
    all_to_all x1, local copies, waits for them, and re-layouts, on_device(): lax.all_to_all(results.reshape(experts, CAP * feat_width), ('expert', 'dp...  24 us
  transfers between devices with their start and end apart: 3, of which 2 were waited for; matrix products, arithmetic and copies ran while one was open for 46% of the time, Pallas kernels for 0%

profile of v1, /device:TPU:0, one launch (start us, length us, event | category | flops | bytes accessed | tf_op | source)
XLA Modules:
  0.0 637.0 jit_solution(18446463856281684283)
XLA Ops:
  7.3 5.9 bitcast_select_fusion
  13.1 10.0 %bitcast_select_fusion.1 = (bf16[4096,768]{1,0:T(8,128)(2,1)}, bf16[4096,768]{1,0:T(8,128)(2,1)}) fusion(bf16[1,4096,768]{2,1,0:T(8,128)(2,1)} %param.9, pred[]{:T(512)S(6)} %eq.59, bf16[1,4096,768]{2,1,0:T(8,128)(2,1)} %param.8), kind=kLoop, calls=%fused_computation.4 | loop fusion | flops 6291456 | bytes 25165824 | tf_op jit(solution)/shard_map/hot_weight_broadcast/jit(_where)/select_n | solution.py:29
  24.4 71.1 %all-reduce.7.cloned.1.call-done = (bf16[768,4096]{1,0:T(8,128)(2,1)}, bf16[4096,768]{1,0:T(8,128)(2,1)}, bf16[4096,768]{1,0:T(8,128)(2,1)}) async-done(((bf16[768,4096]{1,0:T(8,128)(2,1)}, bf16[4096,768]{1,0:T(8,128)(2,1)}, bf16[4096,768]{1,0:T(8,128)(2,1)}), (bf16[768,4096]{1,0:T(8,128)(2,1)}, bf16[4096,768]{1,0:T(8,128)(2,1)}, bf16[4096,768]{1,0:T(8,128)(2,1)})) %all-reduce.7.cloned.1.call-update) | async-done | bytes 18874384 | tf_op jit(solution)/shard_map/hot_weight_broadcast/psum | solution.py:29
  97.0 4.4 convolution_convert_fusion
  101.5 23.9 %all_to_all.16 = bf16[128,1,24576]{2,1,0:T(2,128)(2,1)} reshape(bf16[768,4096]{1,0:T(8,128)(2,1)} %convolution_convert_fusion) | data formatting | bytes 12582912 | tf_op jit(solution)/shard_map/dispatch/all_to_all | solution.py:48
  125.8 38.8 %reduce.2 = bf16[128,24576]{1,0:T(8,128)(2,1)} reduce(bf16[128,1,24576]{2,1,0:T(2,128)(2,1)} %all_to_all.16, bf16[]{:T(256)} %broadcast.85), dimensions={1}, to_apply=%all_to_all.16.reduce_sub_computation | reduce | bytes 12582914 | tf_op jit(solution)/shard_map/dispatch/all_to_all | solution.py:48
  164.7 9.5 %reshape.90 = bf16[128,2,12288]{2,1,0:T(2,128)(2,1)} reshape(bf16[128,24576]{1,0:T(8,128)(2,1)} %reduce.2) | data formatting | bytes 12582912
  174.2 90.0 %all_to_all.20 = bf16[128,2,12288]{2,1,0:T(2,128)(2,1)} all-to-all(bf16[128,2,12288]{2,1,0:T(2,128)(2,1)} %reshape.90), channel_id=1, replica_groups=mesh['expert'=64,'dp'=2] {'expert','dp'}, dimensions={0} | all-to-all | bytes 12582912 | tf_op jit(solution)/shard_map/dispatch/all_to_all | solution.py:48
  264.1 33.8 %reshape.91 = bf16[128,1,24576]{2,1,0:T(2,128)(2,1)} reshape(bf16[128,2,12288]{2,1,0:T(2,128)(2,1)} %all_to_all.20) | data formatting | bytes 12582912
  298.0 38.3 %reduce = bf16[128,24576]{1,0:T(8,128)(2,1)} reduce(bf16[128,1,24576]{2,1,0:T(2,128)(2,1)} %reshape.91, bf16[]{:T(256)} %constant.43), dimensions={1}, to_apply=%all_to_all.13.reduce_sub_computation | reduce | bytes 12582914 | tf_op jit(solution)/shard_map/dispatch/all_to_all | solution.py:48
  336.3 11.5 %reshape.86 = bf16[768,4096]{1,0:T(8,128)(2,1)} reshape(bf16[128,24576]{1,0:T(8,128)(2,1)} %reduce) | data formatting | bytes 12582912 | tf_op jit(solution)/shard_map/expert_ffn/reshape | solution.py:50
  347.8 9.4 %fusion.3 = f32[768,768]{1,0:T(8,128)S(1)} fusion(bf16[768,4096]{1,0:T(8,128)(2,1)} %reshape.86, bf16[1,4096,768]{2,1,0:T(8,128)(2,1)} %param.8), kind=kOutput, calls=%fused_computation.8 | convolution fusion | flops 4831838208 | bytes 14942208 | tf_op jit(solution)/shard_map/expert_ffn/dot_general | solution.py:10
  357.2 8.2 %multiply_convert_fusion = bf16[768,768]{1,0:T(8,128)(2,1)S(1)} fusion(f32[768,768]{1,0:T(8,128)S(1)} %fusion.3, bf16[768,4096]{1,0:T(8,128)(2,1)S(1)} %copy-done.1, bf16[1,4096,768]{2,1,0:T(8,128)(2,1)} %param.9), kind=kOutput, calls=%fused_computation.15 | convolution fusion | flops 4835377152 | bytes 16121856 | tf_op jit(solution)/shard_map/expert_ffn/dot_general | solution.py:11
  365.4 7.1 %convolution_convert_fusion.1 = bf16[768,4096]{1,0:T(8,128)(2,1)} fusion(bf16[768,768]{1,0:T(8,128)(2,1)S(1)} %multiply_convert_fusion, bf16[1,768,4096]{2,1,0:T(8,128)(2,1)S(1)} %bitcast.50), kind=kOutput, calls=%fused_computation.1 | convolution fusion | flops 4834983936 | bytes 13762560 | tf_op jit(solution)/shard_map/expert_ffn/dot_general | solution.py:13
  372.5 24.0 %all_to_all.17 = bf16[128,1,24576]{2,1,0:T(2,128)(2,1)} reshape(bf16[768,4096]{1,0:T(8,128)(2,1)} %convolution_convert_fusion.1) | data formatting | bytes 12582912 | tf_op jit(solution)/shard_map/return/all_to_all | solution.py:52
  396.5 38.8 %reduce.3 = bf16[128,24576]{1,0:T(8,128)(2,1)} reduce(bf16[128,1,24576]{2,1,0:T(2,128)(2,1)} %all_to_all.17, bf16[]{:T(256)} %broadcast.85), dimensions={1}, to_apply=%all_to_all.17.reduce_sub_computation | reduce | bytes 12582914 | tf_op jit(solution)/shard_map/return/all_to_all | solution.py:52
  435.3 9.4 %reshape.92 = bf16[128,2,12288]{2,1,0:T(2,128)(2,1)} reshape(bf16[128,24576]{1,0:T(8,128)(2,1)} %reduce.3) | data formatting | bytes 12582912
  444.7 8.5 %all-to-all-start.1 = ((bf16[128,2,12288]{2,1,0:T(2,128)(2,1)}), bf16[128,2,12288]{2,1,0:T(2,128)(2,1)}, u32[]{:S(2)}, u32[]{:S(2)}) async-start(bf16[128,2,12288]{2,1,0:T(2,128)(2,1)} %reshape.92), calls=%async_computation.1 | async-start | bytes 12582912 | tf_op jit(solution)/shard_map/return/all_to_all | solution.py:52
  454.1 74.8 %all-to-all-done.1 = bf16[128,2,12288]{2,1,0:T(2,128)(2,1)} async-done(((bf16[128,2,12288]{2,1,0:T(2,128)(2,1)}), bf16[128,2,12288]{2,1,0:T(2,128)(2,1)}, u32[]{:S(2)}, u32[]{:S(2)}) %all-to-all-start.1) | async-done | bytes 6291488 | tf_op jit(solution)/shard_map/return/all_to_all | solution.py:52
  528.9 33.8 %reshape.93 = bf16[128,1,24576]{2,1,0:T(2,128)(2,1)} reshape(bf16[128,2,12288]{2,1,0:T(2,128)(2,1)} %all-to-all-done.1) | data formatting | bytes 12582912
  562.7 38.3 %reduce.1 = bf16[128,24576]{1,0:T(8,128)(2,1)} reduce(bf16[128,1,24576]{2,1,0:T(2,128)(2,1)} %reshape.93, bf16[]{:T(256)} %constant.43), dimensions={1}, to_apply=%all_to_all.15.reduce_sub_computation | reduce | bytes 12582914 | tf_op jit(solution)/shard_map/return/all_to_all | solution.py:52
  601.0 11.1 %reshape.87 = bf16[768,4096]{1,0:T(8,128)(2,1)} reshape(bf16[128,24576]{1,0:T(8,128)(2,1)} %reduce.1) | data formatting | bytes 12582912 | tf_op jit(solution)/shard_map/return/reshape | solution.py:55
  616.0 7.2 %fusion.7 = f32[96,4096]{1,0:T(8,128)S(1)} fusion(bf16[768,4096]{1,0:T(8,128)(2,1)} %get-tuple-element.5, bf16[96,4096]{1,0:T(8,128)(2,1)S(1)} %copy-done, bf16[4096,768]{1,0:T(8,128)(2,1)} %get-tuple-element.6, f32[96]{0:T(128)S(1)} %get-tuple-element.12, f32[96,768]{1,0:T(8,128)S(1)} %convolution_bitcast_fusion.1), kind=kOutput, calls=%fused_computation.14 | convolution fusion | flops 1209581568 | bytes 15237504 | tf_op jit(solution)/shard_map/hot_expert/dot_general | solution.py:13
  623.2 6.8 %fusion.5 = bf16[96,4096]{1,0:T(8,128)(2,1)} fusion(f32[96,4096]{1,0:T(8,128)S(1)} %fusion.7, f32[768,96]{0,1:T(8,128)S(1)} %select_reduce_fusion, bf16[768,4096]{1,0:T(8,128)(2,1)} %reshape.87), kind=kOutput, calls=%fused_computation.11 | convolution fusion | flops 3624665088 | bytes 8945664 | tf_op jit(solution)/shard_map/combine/dot_general | solution.py:61
  (38 shorter events, 8.0 us)
Async XLA Ops:
  6.5 90.5 %copy-start = (bf16[96,4096]{1,0:T(8,128)(2,1)S(1)}, bf16[96,4096]{1,0:T(8,128)(2,1)}, u32[]{:S(2)}) copy-start(bf16[96,4096]{1,0:T(8,128)(2,1)} %param.7) | copy-start | bytes 2359300
  6.5 88.9 %all-reduce.7.cloned.1.call-start = ((), (), s32[]{:S(2)}) async-start(), calls=%async_computation.3 | async-start | bytes 37748736 | tf_op jit(solution)/shard_map/hot_weight_broadcast/psum | solution.py:29
  23.1 0.7 copy-start.2
  23.2 588.9 %all-reduce.5.cloned.1.call-start = ((), (), s32[]{:S(2)}) async-start(), calls=%async_computation.2 | async-start | bytes 37748736 | tf_op jit(solution)/shard_map/hot_weight_broadcast/psum | solution.py:29
  336.3 29.1 %slice-start = ((s8[6291456]{0:T(1024)(128)(4,1)}), s8[2097152]{0:T(1024)(128)(4,1)S(1)}, s32[]{:S(2)}) async-start(s8[6291456]{0:T(1024)(128)(4,1)} %bitcast.49), calls=%async_computation.4 | async-start | bytes 4194304
  347.8 9.4 %copy-start.1 = (bf16[768,4096]{1,0:T(8,128)(2,1)S(1)}, bf16[768,4096]{1,0:T(8,128)(2,1)}, u32[]{:S(2)}) copy-start(bf16[768,4096]{1,0:T(8,128)(2,1)} %reshape.86) | copy-start | bytes 18874372
  347.8 17.6 %slice-start.1 = ((s8[6291456]{0:T(1024)(128)(4,1)}), s8[4194304]{0:T(1024)(128)(4,1)S(1)}, s32[]{:S(2)}) async-start(s8[6291456]{0:T(1024)(128)(4,1)} %bitcast.49), calls=%async_computation.5 | async-start | bytes 8388608
  444.7 8.5 %copy-start.3 = (f32[96,8]{0,1:T(8,128)S(1)}, f32[96,8]{0,1:T(8,128)}, u32[]{:S(2)}) copy-start(f32[96,8]{0,1:T(8,128)} %param.12) | copy-start | bytes 9220
  444.7 84.2 %all-to-all-start.1 = ((bf16[128,2,12288]{2,1,0:T(2,128)(2,1)}), bf16[128,2,12288]{2,1,0:T(2,128)(2,1)}, u32[]{:S(2)}, u32[]{:S(2)}) async-start(bf16[128,2,12288]{2,1,0:T(2,128)(2,1)} %reshape.92), calls=%async_computation.1 | async-start | bytes 12582912 | tf_op jit(solution)/shard_map/return/all_to_all | solution.py:52
Sparse Core Ops, SparseCore 0:
  23.3 72.0 all-reduce.6
  102.7 296.8 all-reduce.4
